TPU v7x, 256 devices: a whole 4x4x8 slice. The times are simulated.
256 devices in a mesh: leaf: 16 (over z, core), list: 16 (over y, x).
Axes of the slice: x: 4, y: 4, z: 8, core: 2. Of those that a mesh axis runs over, the one named last changes fastest.
Arguments:
- panel_charges: bfloat16 [4096, 64, 256], P(('leaf', 'list')), may hold values from -6 to 6
- leaf_basis: bfloat16 [4096, 64, 256], P(('leaf', 'list')), may hold values from -0.375 to 0.375
- near_blocks: bfloat16 [4096, 4, 256, 256], P(('leaf', 'list')), may hold values from -0.1875 to 0.1875
- near_list: int32 [4096, 4], P(('leaf', 'list')), may hold values from 0 to 15, as said below
- far_list: int32 [4096, 8], P(('leaf', 'list')), may hold values from 0 to 255, as said below
- far_count: int32 [4096], P(('leaf', 'list')), may hold values from 1 to 8, as said below
- far_coupling: bfloat16 [4096, 8, 64, 64], P(('leaf', 'list')), may hold values from -0.25 to 0.25
- leaf_transfer: float32 [4096, 64, 64], P(('leaf', 'list')), may hold values from -0.4375 to 0.4375
- device_transfer: float32 [16, 16, 64, 64], P('leaf', 'list'), may hold values from -0.375 to 0.375
- tree_transfer: float32 [24, 64, 64], replicated, may hold values from -0.75 to 0.75
- level_coupling: float32 [28, 4, 64, 64], replicated, may hold values from -0.4375 to 0.4375
Outputs:
- potential: bfloat16 [4096, 64, 256], P(('leaf', 'list'))
Inputs may be any that keep to these rules, and one draw needn't show every extreme that they name: `far_list`: each row names 8 different leaves of the leaf's group subtree, none on the leaf's own device; the 16 leaves of one device name, over all their slots, exactly 8 different leaves of each other device of the group. Slots at and after far_count[c] are unused. `near_list`: each row names 4 different leaves of the leaf's own device, the first being the leaf itself.
All inputs are finite; a program needn't handle non-finite values.
Results may differ from a plain program's by a relative error of at most 0.0053.
Values may be sent and summed in bfloat16 or wider, within the bound.
A program may use at most 64 MiB of HBM per device.

v0:
```python
import jax
import jax.numpy as jnp
from jax import lax
from jax.sharding import PartitionSpec as P

highest = lax.Precision.HIGHEST
offsets = (-3, -2, 2, 3)


def partner(array, axis, distance):
    return lax.ppermute(array, axis, [(i, i ^ 1 << distance) for i in range(lax.axis_size(axis))])


def shifted(array, axis, by):
    length = lax.axis_size(axis)
    pairs = [(i, i + by) for i in range(length) if 0 <= i + by < length]
    return lax.ppermute(array, axis, pairs)


def pick_usable(offset, parity):
    if offset == 3:
        return parity == 0
    if offset == -3:
        return parity == 1
    return parity >= 0


def upper_exchange(group_node, tree_transfer, level_coupling):
    leaf_count = lax.axis_size("leaf")
    depth = leaf_count.bit_length() - 2
    position = lax.axis_index("leaf")
    nodes = [group_node]
    for height in range(depth - 1):
        begin_row = 2 * leaf_count - 2 * (leaf_count >> height)
        matrix = tree_transfer[begin_row + (position >> height)]
        own_part = jnp.dot(nodes[-1], matrix, precision=highest)
        nodes.append(own_part + partner(own_part, "leaf", height))
    coupled = []
    for height in range(depth):
        begin_row = 2 * leaf_count - 2 * (leaf_count >> height)
        matrices = level_coupling[begin_row + (position >> height)]
        parity = (position >> height) % 2
        summed = jnp.zeros_like(group_node)
        for slot_index, offset in enumerate(offsets):
            source = shifted(nodes[height], "leaf", -offset * (1 << height))
            contribution = jnp.dot(source, matrices[slot_index].T, precision=highest)
            summed = summed + jnp.where(
                pick_usable(offset, parity), contribution, jnp.zeros((), jnp.float32)
            )
        coupled.append(summed)
    result = coupled[-1]
    for height in reversed(range(depth - 1)):
        begin_row = 2 * leaf_count - 2 * (leaf_count >> height)
        matrix = tree_transfer[begin_row + (position >> height)]
        result = coupled[height] + jnp.dot(result, matrix.T, precision=highest)
    return result


def on_device(
    panel_charges,
    leaf_basis,
    near_blocks,
    near_list,
    far_list,
    far_count,
    far_coupling,
    leaf_transfer,
    device_transfer,
    tree_transfer,
    level_coupling,
):
    leaf_local = panel_charges.shape[0]
    far_slots = far_list.shape[1]
    near_slots = near_list.shape[1]
    skeleton = jnp.einsum(
        "crm,ckm->crk", panel_charges, leaf_basis, preferred_element_type=jnp.float32
    ).astype(jnp.bfloat16)
    device_node = jnp.einsum(
        "irb,iba->ra", skeleton.astype(jnp.float32), leaf_transfer, precision=highest
    )
    device_term = jnp.dot(device_node, device_transfer[0, 0], precision=highest)
    group_node = lax.psum(device_term, "list")
    top_down = upper_exchange(group_node, tree_transfer, level_coupling)
    device_down = jnp.dot(top_down, device_transfer[0, 0].T, precision=highest)
    from_above = jnp.einsum("rd,ild->irl", device_down, leaf_transfer, precision=highest)
    row_width = skeleton.shape[1] * skeleton.shape[2]
    flattened = skeleton.reshape(leaf_local, row_width)
    wanted = far_list.reshape(-1)
    usable = (jnp.arange(far_slots, dtype=jnp.int32)[None, :] < far_count[:, None]).reshape(-1)
    piece = lax.all_gather(flattened, "list", axis=0, tiled=True)
    columns = jnp.arange(piece.shape[0], dtype=jnp.int32)
    hits = ((wanted[:, None] == columns[None, :]) & usable[:, None]).astype(jnp.bfloat16)
    collected = jnp.dot(hits, piece, preferred_element_type=jnp.float32)
    selected = collected.astype(jnp.bfloat16)
    selected = selected.reshape(leaf_local, far_slots, skeleton.shape[1], skeleton.shape[2])
    leaf_coupled = jnp.einsum(
        "ckrb,ckab->cra", selected, far_coupling, preferred_element_type=jnp.float32
    )
    coefficients = (leaf_coupled + from_above).astype(jnp.bfloat16)
    far_field = jnp.einsum(
        "crk,ckm->crm", coefficients, leaf_basis, preferred_element_type=jnp.float32
    )
    neighbours = jnp.take(panel_charges, near_list.reshape(-1), axis=0)
    neighbours = neighbours.reshape(
        leaf_local, near_slots, panel_charges.shape[1], panel_charges.shape[2]
    )
    near_field = jnp.einsum(
        "ckrm,cknm->crn", neighbours, near_blocks, preferred_element_type=jnp.float32
    )
    return (far_field + near_field).astype(jnp.bfloat16)


def solution(mesh):
    in_specs = (
        P(("leaf", "list"), None, None),
        P(("leaf", "list"), None, None),
        P(("leaf", "list"), None, None, None),
        P(("leaf", "list"), None),
        P(("leaf", "list"), None),
        P(("leaf", "list")),
        P(("leaf", "list"), None, None, None),
        P(("leaf", "list"), None, None),
        P("leaf", "list", None, None),
        P(),
        P(),
    )
    out_specs = P(("leaf", "list"), None, None)
    return jax.shard_map(
        on_device, mesh=mesh, in_specs=in_specs, out_specs=out_specs, check_vma=False
    )
```

profile of v0, /device:TPU:32, one launch (start us, length us, event | category | flops | bytes accessed | tf_op | source)
XLA Modules:
  0.0 177.3 jit_solution(7116425798900764517)
XLA Ops:
  6.5 1.6 convolution_convert_fusion.1
  8.2 1.4 convolution_bitcast_fusion.3
  10.5 74.6 %psum.7 = f32[64,64]{1,0:T(8,128)S(1)} all-reduce(f32[64,64]{1,0:T(8,128)S(1)} %fusion.34), channel_id=1, replica_groups=mesh['leaf'=16,'list'=16] {'list'}, use_global_device_ids=true, to_apply=%region_0.0 | all-reduce | flops 4096 | bytes 32768 | tf_op jit(solution)/shard_map/psum | solution.py:82
  85.1 1.3 collective-permute-start.3
  86.4 2.0 %collective-permute-start.2 = (f32[64,64]{1,0:T(8,128)S(1)}, f32[64,64]{1,0:T(8,128)S(1)}, u32[]{:S(2)}, u32[]{:S(2)}) collective-permute-start(f32[64,64]{1,0:T(8,128)S(1)} %psum.7), channel_id=1, source_target_pairs={{32,0},{48,16},{64,32},{80,48},{96,64},{112,80},{128,96},{144,112}... | collective-permute-start | bytes 49160 | tf_op jit(solution)/shard_map/ppermute | solution.py:17
  88.5 4.3 %collective-permute-start.1 = (f32[64,64]{1,0:T(8,128)S(1)}, f32[64,64]{1,0:T(8,128)S(1)}, u32[]{:S(2)}, u32[]{:S(2)}) collective-permute-start(f32[64,64]{1,0:T(8,128)S(1)} %psum.7), channel_id=1, source_target_pairs={{0,32},{16,48},{32,64},{48,80},{64,96},{80,112},{96,128},{112,144}... | collective-permute-start | bytes 49160 | tf_op jit(solution)/shard_map/ppermute | solution.py:17
  92.8 3.4 %collective-permute-start = (f32[64,64]{1,0:T(8,128)S(1)}, f32[64,64]{1,0:T(8,128)S(1)}, u32[]{:S(2)}, u32[]{:S(2)}) collective-permute-start(f32[64,64]{1,0:T(8,128)S(1)} %psum.7), channel_id=1, source_target_pairs={{0,48},{16,64},{32,80},{48,96},{64,112},{80,128},{96,144},{112,160... | collective-permute-start | bytes 49160 | tf_op jit(solution)/shard_map/ppermute | solution.py:17
  98.1 3.3 %collective-permute-start.4 = (f32[64,64]{1,0:T(8,128)S(1)}, f32[64,64]{1,0:T(8,128)S(1)}, u32[]{:S(2)}, u32[]{:S(2)}) collective-permute-start(f32[64,64]{1,0:T(8,128)S(1)} %fusion.31), channel_id=1, source_target_pairs={{0,16},{16,0},{32,48},{48,32},{64,80},{80,64},{96,112},{112,96},{1... | collective-permute-start | bytes 49160 | tf_op jit(solution)/shard_map/ppermute | solution.py:11
  103.1 2.0 %gather_fusion = bf16[64,64,256]{2,1,0:T(8,128)(2,1)} fusion(bf16[16,64,256]{2,1,0:T(8,128)(2,1)S(1)} %copy-done.1, s32[1024]{0:T(1024)S(1)} %pad_clamp_fusion), kind=kCustom, calls=%fused_computation | custom fusion | bytes 4194560 | tf_op jit(solution)/shard_map/jit(_take)/gather | solution.py:103
  105.1 6.8 %fusion.3 = f32[16,64,256]{2,1,0:T(8,128)S(1)} fusion(bf16[16,4,256,256]{3,2,1,0:T(8,128)(2,1)} %param.13, bf16[16,4,64,256]{3,2,1,0:T(8,128)(2,1)} %bitcast.100, pred[16,4]{1,0:T(8,128)(4,1)S(1)} %copy.16), kind=kOutput, calls=%fused_computation.5 | convolution fusion | flops 537919488 | bytes 11534400 | tf_op jit(solution)/shard_map/ckrm,cknm->crn/dot_general | solution.py:107
  112.3 1.3 collective-permute-start.8
  114.5 1.3 collective-permute-start.7
  116.8 5.5 %collective-permute-start.6 = (f32[64,64]{1,0:T(8,128)S(1)}, f32[64,64]{1,0:T(8,128)S(1)}, u32[]{:S(2)}, u32[]{:S(2)}) collective-permute-start(f32[64,64]{1,0:T(8,128)S(1)} %add.117), channel_id=1, source_target_pairs={{0,64},{16,80},{32,96},{48,112},{64,128},{80,144},{96,160},{112,17... | collective-permute-start | bytes 49160 | tf_op jit(solution)/shard_map/ppermute | solution.py:17
  124.7 2.6 %collective-permute-done.9 = f32[64,64]{1,0:T(8,128)S(1)} collective-permute-done((f32[64,64]{1,0:T(8,128)S(1)}, f32[64,64]{1,0:T(8,128)S(1)}, u32[]{:S(2)}, u32[]{:S(2)}) %collective-permute-start.9) | collective-permute-done | bytes 16416 | tf_op jit(solution)/shard_map/ppermute | solution.py:11
  127.3 7.4 %collective-permute-start.5 = (f32[64,64]{1,0:T(8,128)S(1)}, f32[64,64]{1,0:T(8,128)S(1)}, u32[]{:S(2)}, u32[]{:S(2)}) collective-permute-start(f32[64,64]{1,0:T(8,128)S(1)} %add.117), channel_id=1, source_target_pairs={{0,96},{16,112},{32,128},{48,144},{64,160},{80,176},{96,192},{112,... | collective-permute-start | bytes 49160 | tf_op jit(solution)/shard_map/ppermute | solution.py:17
  134.8 1.3 collective-permute-start.13
  137.1 1.3 collective-permute-start.12
  139.3 8.5 %collective-permute-start.11 = (f32[64,64]{1,0:T(8,128)S(1)}, f32[64,64]{1,0:T(8,128)S(1)}, u32[]{:S(2)}, u32[]{:S(2)}) collective-permute-start(f32[64,64]{1,0:T(8,128)S(1)} %add.125), channel_id=1, source_target_pairs={{0,128},{16,144},{32,160},{48,176},{64,192},{80,208},{96,224},{112... | collective-permute-start | bytes 49160 | tf_op jit(solution)/shard_map/ppermute | solution.py:17
  148.8 1.3 collective-permute-start.10
  158.0 3.1 %convolution_convert_fusion = bf16[128,4096]{1,0:T(8,128)(2,1)} fusion(bf16[256,4096]{1,0:T(8,128)(2,1)} %all-gather.2.cloned.1.call-done, s32[128]{0:T(128)S(1)} %eq.37, pred[128]{0:T(512)(128)(4,1)S(1)} %lt.70), kind=kOutput, calls=%fused_computation.1 | convolution fusion | flops 269025280 | bytes 3146368 | tf_op jit(solution)/shard_map/dot_general | solution.py:93
  161.1 4.3 %reshape.87 = bf16[16,8,64,64]{3,2,1,0:T(8,128)(2,1)} reshape(bf16[128,4096]{1,0:T(8,128)(2,1)} %convolution_convert_fusion) | data formatting | bytes 2097152 | tf_op jit(solution)/shard_map/reshape | solution.py:95
  165.3 2.4 %convolution_bitcast_fusion = f32[16,64,64]{2,1,0:T(8,128)S(1)} fusion(bf16[16,8,64,64]{3,2,1,0:T(8,128)(2,1)} %reshape.87, bf16[16,8,64,64]{3,2,1,0:T(8,128)(2,1)S(1)} %copy-done), kind=kOutput, calls=%fused_computation.8 | convolution fusion | flops 67108864 | bytes 2359296 | tf_op jit(solution)/shard_map/ckrb,ckab->cra/dot_general | solution.py:96
  167.7 1.6 fusion.8
  169.3 1.1 fusion.6
  (62 shorter events, 19.7 us)
Async XLA Ops:
  6.5 158.8 %copy-start = (bf16[16,8,64,64]{3,2,1,0:T(8,128)(2,1)S(1)}, bf16[16,8,64,64]{3,2,1,0:T(8,128)(2,1)}, u32[]{:S(2)}) copy-start(bf16[16,8,64,64]{3,2,1,0:T(8,128)(2,1)} %param.17) | copy-start | bytes 3145732
  6.5 96.5 %copy-start.1 = (bf16[16,64,256]{2,1,0:T(8,128)(2,1)S(1)}, bf16[16,64,256]{2,1,0:T(8,128)(2,1)}, u32[]{:S(2)}) copy-start(bf16[16,64,256]{2,1,0:T(8,128)(2,1)} %param.11) | copy-start | bytes 1572868
  6.5 151.5 %all-gather.2.cloned.1.call-start = ((), (), s32[]{:S(2)}) async-start(), calls=%async_computation | async-start | bytes 2228224 | tf_op jit(solution)/shard_map/all_gather | solution.py:90
  85.1 38.2 %collective-permute-start.3 = (f32[64,64]{1,0:T(8,128)S(1)}, f32[64,64]{1,0:T(8,128)S(1)}, u32[]{:S(2)}, u32[]{:S(2)}) collective-permute-start(f32[64,64]{1,0:T(8,128)S(1)} %psum.7), channel_id=1, source_target_pairs={{48,0},{64,16},{80,32},{96,48},{112,64},{128,80},{144,96},{160,112... | collective-permute-start | bytes 49160 | tf_op jit(solution)/shard_map/ppermute | solution.py:17
  86.4 28.1 %collective-permute-start.2 = (f32[64,64]{1,0:T(8,128)S(1)}, f32[64,64]{1,0:T(8,128)S(1)}, u32[]{:S(2)}, u32[]{:S(2)}) collective-permute-start(f32[64,64]{1,0:T(8,128)S(1)} %psum.7), channel_id=1, source_target_pairs={{32,0},{48,16},{64,32},{80,48},{96,64},{112,80},{128,96},{144,112}... | collective-permute-start | bytes 49160 | tf_op jit(solution)/shard_map/ppermute | solution.py:17
  88.5 28.3 %collective-permute-start.1 = (f32[64,64]{1,0:T(8,128)S(1)}, f32[64,64]{1,0:T(8,128)S(1)}, u32[]{:S(2)}, u32[]{:S(2)}) collective-permute-start(f32[64,64]{1,0:T(8,128)S(1)} %psum.7), channel_id=1, source_target_pairs={{0,32},{16,48},{32,64},{48,80},{64,96},{80,112},{96,128},{112,144}... | collective-permute-start | bytes 49160 | tf_op jit(solution)/shard_map/ppermute | solution.py:17
  92.8 64.0 %collective-permute-start = (f32[64,64]{1,0:T(8,128)S(1)}, f32[64,64]{1,0:T(8,128)S(1)}, u32[]{:S(2)}, u32[]{:S(2)}) collective-permute-start(f32[64,64]{1,0:T(8,128)S(1)} %psum.7), channel_id=1, source_target_pairs={{0,48},{16,64},{32,80},{48,96},{64,112},{80,128},{96,144},{112,160... | collective-permute-start | bytes 49160 | tf_op jit(solution)/shard_map/ppermute | solution.py:17
  98.1 14.2 %collective-permute-start.4 = (f32[64,64]{1,0:T(8,128)S(1)}, f32[64,64]{1,0:T(8,128)S(1)}, u32[]{:S(2)}, u32[]{:S(2)}) collective-permute-start(f32[64,64]{1,0:T(8,128)S(1)} %fusion.31), channel_id=1, source_target_pairs={{0,16},{16,0},{32,48},{48,32},{64,80},{80,64},{96,112},{112,96},{1... | collective-permute-start | bytes 49160 | tf_op jit(solution)/shard_map/ppermute | solution.py:11
  105.1 6.9 %copy-start.6 = (s32[16]{0:T(128)S(1)}, s32[16]{0:T(128)}, u32[]{:S(2)}) copy-start(s32[16]{0:T(128)} %param.16) | copy-start | bytes 196
  105.1 7.0 %copy-start.5 = (s32[16,8]{0,1:T(8,128)S(1)}, s32[16,8]{0,1:T(8,128)}, u32[]{:S(2)}) copy-start(s32[16,8]{0,1:T(8,128)} %param.15) | copy-start | bytes 1540
  105.1 52.7 %copy-start.4 = (f32[1,1,64,64]{3,2,1,0:T(8,128)S(1)}, f32[1,1,64,64]{3,2,1,0:T(8,128)}, u32[]{:S(2)}) copy-start(f32[1,1,64,64]{3,2,1,0:T(8,128)} %param.19) | copy-start | bytes 49156
  112.3 27.0 %collective-permute-start.8 = (f32[64,64]{1,0:T(8,128)S(1)}, f32[64,64]{1,0:T(8,128)S(1)}, u32[]{:S(2)}, u32[]{:S(2)}) collective-permute-start(f32[64,64]{1,0:T(8,128)S(1)} %add.117), channel_id=1, source_target_pairs={{96,0},{112,16},{128,32},{144,48},{160,64},{176,80},{192,96},{208,... | collective-permute-start | bytes 49160 | tf_op jit(solution)/shard_map/ppermute | solution.py:17
  114.5 20.3 %collective-permute-start.7 = (f32[64,64]{1,0:T(8,128)S(1)}, f32[64,64]{1,0:T(8,128)S(1)}, u32[]{:S(2)}, u32[]{:S(2)}) collective-permute-start(f32[64,64]{1,0:T(8,128)S(1)} %add.117), channel_id=1, source_target_pairs={{64,0},{80,16},{96,32},{112,48},{128,64},{144,80},{160,96},{176,11... | collective-permute-start | bytes 49160 | tf_op jit(solution)/shard_map/ppermute | solution.py:17
  116.8 20.3 %collective-permute-start.6 = (f32[64,64]{1,0:T(8,128)S(1)}, f32[64,64]{1,0:T(8,128)S(1)}, u32[]{:S(2)}, u32[]{:S(2)}) collective-permute-start(f32[64,64]{1,0:T(8,128)S(1)} %add.117), channel_id=1, source_target_pairs={{0,64},{16,80},{32,96},{48,112},{64,128},{80,144},{96,160},{112,17... | collective-permute-start | bytes 49160 | tf_op jit(solution)/shard_map/ppermute | solution.py:17
  123.3 4.0 %collective-permute-start.9 = (f32[64,64]{1,0:T(8,128)S(1)}, f32[64,64]{1,0:T(8,128)S(1)}, u32[]{:S(2)}, u32[]{:S(2)}) collective-permute-start(f32[64,64]{1,0:T(8,128)S(1)} %fusion.27), channel_id=1, source_target_pairs={{0,32},{16,48},{32,0},{48,16},{64,96},{80,112},{96,64},{112,80},{1... | collective-permute-start | bytes 49160 | tf_op jit(solution)/shard_map/ppermute | solution.py:11
  127.3 27.6 %collective-permute-start.5 = (f32[64,64]{1,0:T(8,128)S(1)}, f32[64,64]{1,0:T(8,128)S(1)}, u32[]{:S(2)}, u32[]{:S(2)}) collective-permute-start(f32[64,64]{1,0:T(8,128)S(1)} %add.117), channel_id=1, source_target_pairs={{0,96},{16,112},{32,128},{48,144},{64,160},{80,176},{96,192},{112,... | collective-permute-start | bytes 49160 | tf_op jit(solution)/shard_map/ppermute | solution.py:17
  134.8 17.2 %collective-permute-start.13 = (f32[64,64]{1,0:T(8,128)S(1)}, f32[64,64]{1,0:T(8,128)S(1)}, u32[]{:S(2)}, u32[]{:S(2)}) collective-permute-start(f32[64,64]{1,0:T(8,128)S(1)} %add.125), channel_id=1, source_target_pairs={{192,0},{208,16},{224,32},{240,48},{193,1},{209,17},{225,33},{241,... | collective-permute-start | bytes 49160 | tf_op jit(solution)/shard_map/ppermute | solution.py:17
  137.1 11.7 %collective-permute-start.12 = (f32[64,64]{1,0:T(8,128)S(1)}, f32[64,64]{1,0:T(8,128)S(1)}, u32[]{:S(2)}, u32[]{:S(2)}) collective-permute-start(f32[64,64]{1,0:T(8,128)S(1)} %add.125), channel_id=1, source_target_pairs={{128,0},{144,16},{160,32},{176,48},{192,64},{208,80},{224,96},{240... | collective-permute-start | bytes 49160 | tf_op jit(solution)/shard_map/ppermute | solution.py:17
  139.3 11.7 %collective-permute-start.11 = (f32[64,64]{1,0:T(8,128)S(1)}, f32[64,64]{1,0:T(8,128)S(1)}, u32[]{:S(2)}, u32[]{:S(2)}) collective-permute-start(f32[64,64]{1,0:T(8,128)S(1)} %add.125), channel_id=1, source_target_pairs={{0,128},{16,144},{32,160},{48,176},{64,192},{80,208},{96,224},{112... | collective-permute-start | bytes 49160 | tf_op jit(solution)/shard_map/ppermute | solution.py:17
  148.8 4.2 %collective-permute-start.10 = (f32[64,64]{1,0:T(8,128)S(1)}, f32[64,64]{1,0:T(8,128)S(1)}, u32[]{:S(2)}, u32[]{:S(2)}) collective-permute-start(f32[64,64]{1,0:T(8,128)S(1)} %add.125), channel_id=1, source_target_pairs={{0,192},{16,208},{32,224},{48,240},{1,193},{17,209},{33,225},{49,2... | collective-permute-start | bytes 49160 | tf_op jit(solution)/shard_map/ppermute | solution.py:17
  165.3 2.4 %copy-start.2 = (f32[16,64,64]{2,1,0:T(8,128)S(1)}, f32[16,64,64]{2,1,0:T(8,128)}, u32[]{:S(2)}) copy-start(f32[16,64,64]{2,1,0:T(8,128)} %param.18) | copy-start | bytes 786436
  165.3 4.0 %copy-start.3 = (bf16[16,64,256]{2,1,0:T(8,128)(2,1)S(1)}, bf16[16,64,256]{2,1,0:T(8,128)(2,1)}, u32[]{:S(2)}) copy-start(bf16[16,64,256]{2,1,0:T(8,128)(2,1)} %param.12) | copy-start | bytes 1572868
Sparse Core Ops, SparseCore 0:
  97.3 47.2 all-gather.1
where the time goes:
time: 179 us; the launch traced here: 177 us
  blocking collectives  74.6 us (42%)
  starting transfers between devices  42.7 us (24%)
  matrix products  34.2 us (19%)
  between operations  13.8 us (8%)
  local copies, waits for them, and re-layouts  8.41 us (5%)
  waiting for transfers between devices  2.66 us (1%)
    psum x1, blocking collectives, on_device(): group_node = lax.psum(device_term, 'list')  74.6 us
    ppermute x12, starting transfers between devices, shifted(): return lax.ppermute(array, axis, pairs)  38.9 us
    dot_general x12, matrix products, upper_exchange(): contribution = jnp.dot(source, matrices[slot_index].T, precision=highest)  11.4 us
    dot_general x1, matrix products, on_device(): jnp.einsum('ckrm,cknm->crn', neighbours, near_blocks, preferred_element_t...  6.84 us
    reshape x1, local copies, waits for them, and re-layouts, on_device(): selected.reshape(leaf_local, far_slots, skeleton.shape[1], skeleton.shape...  4.26 us
    ppermute x2, starting transfers between devices, partner(): lax.ppermute(array, axis, [(i, i ^ 1 << distance) for i in range(lax.axis...  3.79 us
  transfers between devices with their start and end apart: 15, of which 1 were waited for; matrix products, arithmetic and copies ran while one was open for 15% of the time, Pallas kernels for 0%

commit v1 on v0

--- a/solution.py
+++ b/solution.py
@@ -79,7 +79,7 @@
         "irb,iba->ra", skeleton.astype(jnp.float32), leaf_transfer, precision=highest
     )
     device_term = jnp.dot(device_node, device_transfer[0, 0], precision=highest)
-    group_node = lax.psum(device_term, "list")
+    group_node = jnp.sum(lax.all_gather(device_term, "list"), 0)
     top_down = upper_exchange(group_node, tree_transfer, level_coupling)
     device_down = jnp.dot(top_down, device_transfer[0, 0].T, precision=highest)
     from_above = jnp.einsum("rd,ild->irl", device_down, leaf_transfer, precision=highest)

time: 179 us -> 130 us (0.73)
  blocking collectives: 74.6 us -> 26.2 us
    psum x1 -> x0, blocking collectives: 74.6 us -> none  [on_device(): group_node = lax.psum(device_term, 'list')]
    all_gather x0 -> x1, blocking collectives: none -> 26.2 us  [on_device(): group_node = jnp.sum(lax.all_gather(device_term, 'list'), 0)]
  transfers between devices with their start and end apart: 15 -> 15, of which waited for: 1 -> 1; matrix products, arithmetic and copies ran while one was open for 15% -> 20% of each run, Pallas kernels for 0% -> 0%
where the time goes in v1:
time: 130 us; the launch traced here: 129 us
  starting transfers between devices  42.7 us (33%)
  matrix products  34.1 us (26%)
  blocking collectives  26.2 us (20%)
  between operations  13.8 us (11%)
  local copies, waits for them, and re-layouts  7.73 us (6%)
  waiting for transfers between devices  2.66 us (2%)
    ppermute x12, starting transfers between devices, shifted(): return lax.ppermute(array, axis, pairs)  38.9 us
    all_gather x1, blocking collectives, on_device(): group_node = jnp.sum(lax.all_gather(device_term, 'list'), 0)  26.2 us
    dot_general x12, matrix products, upper_exchange(): contribution = jnp.dot(source, matrices[slot_index].T, precision=highest)  11.4 us
    dot_general x1, matrix products, on_device(): jnp.einsum('ckrm,cknm->crn', neighbours, near_blocks, preferred_element_t...  6.69 us
    reshape x1, local copies, waits for them, and re-layouts, on_device(): selected.reshape(leaf_local, far_slots, skeleton.shape[1], skeleton.shape...  4.25 us
    ppermute x2, starting transfers between devices, partner(): lax.ppermute(array, axis, [(i, i ^ 1 << distance) for i in range(lax.axis...  3.79 us
    dot_general x1, matrix products, on_device(): collected = jnp.dot(hits, piece, preferred_element_type=jnp.float32)  3.06 us
  transfers between devices with their start and end apart: 15, of which 1 were waited for; matrix products, arithmetic and copies ran while one was open for 20% of the time, Pallas kernels for 0%

profile of v1, /device:TPU:32, one launch (start us, length us, event | category | flops | bytes accessed | tf_op | source)
XLA Modules:
  0.0 128.5 jit_solution(16155438489979381765)
XLA Ops:
  6.5 1.6 %convolution_convert_fusion.1 = bf16[16,64,64]{2,1,0:T(8,128)(2,1)S(1)} fusion(bf16[16,64,256]{2,1,0:T(8,128)(2,1)} %param.11, bf16[16,64,256]{2,1,0:T(8,128)(2,1)} %param.12), kind=kOutput, calls=%fused_computation.12 | convolution fusion | flops 33619968 | bytes 1179648 | tf_op jit(solution)/shard_map/crm,ckm->crk/dot_general | solution.py:75
  8.2 1.4 %convolution_bitcast_fusion.3 = f32[64,64]{1,0:T(8,128)S(1)} fusion(bf16[16,64,64]{2,1,0:T(8,128)(2,1)S(1)} %convolution_convert_fusion.1, f32[16,64,64]{2,1,0:T(8,128)} %param.18), kind=kOutput, calls=%fused_computation.37 | convolution fusion | flops 50331648 | bytes 409600 | tf_op jit(solution)/shard_map/irb,iba->ra/dot_general | solution.py:78
  10.5 26.2 %all-gather = f32[1024,64]{1,0:T(8,128)} all-gather(f32[64,64]{1,0:T(8,128)S(1)} %fusion.34), channel_id=2, replica_groups=mesh['leaf'=16,'list'=16] {'list'}, dimensions={0}, use_global_device_ids=true | all-gather | bytes 278528 | tf_op jit(solution)/shard_map/all_gather | solution.py:82
  36.8 1.1 reduce_sum.9
  37.9 1.3 %collective-permute-start.3 = (f32[64,64]{1,0:T(8,128)S(1)}, f32[64,64]{1,0:T(8,128)S(1)}, u32[]{:S(2)}, u32[]{:S(2)}) collective-permute-start(f32[64,64]{1,0:T(8,128)S(1)} %reduce_sum.9), channel_id=1, source_target_pairs={{48,0},{64,16},{80,32},{96,48},{112,64},{128,80},{144,96},{160,112... | collective-permute-start | bytes 49160 | tf_op jit(solution)/shard_map/ppermute | solution.py:17
  39.2 2.0 %collective-permute-start.2 = (f32[64,64]{1,0:T(8,128)S(1)}, f32[64,64]{1,0:T(8,128)S(1)}, u32[]{:S(2)}, u32[]{:S(2)}) collective-permute-start(f32[64,64]{1,0:T(8,128)S(1)} %reduce_sum.9), channel_id=1, source_target_pairs={{32,0},{48,16},{64,32},{80,48},{96,64},{112,80},{128,96},{144,112}... | collective-permute-start | bytes 49160 | tf_op jit(solution)/shard_map/ppermute | solution.py:17
  41.2 4.4 %collective-permute-start.1 = (f32[64,64]{1,0:T(8,128)S(1)}, f32[64,64]{1,0:T(8,128)S(1)}, u32[]{:S(2)}, u32[]{:S(2)}) collective-permute-start(f32[64,64]{1,0:T(8,128)S(1)} %reduce_sum.9), channel_id=1, source_target_pairs={{0,32},{16,48},{32,64},{48,80},{64,96},{80,112},{96,128},{112,144}... | collective-permute-start | bytes 49160 | tf_op jit(solution)/shard_map/ppermute | solution.py:17
  45.6 3.4 %collective-permute-start = (f32[64,64]{1,0:T(8,128)S(1)}, f32[64,64]{1,0:T(8,128)S(1)}, u32[]{:S(2)}, u32[]{:S(2)}) collective-permute-start(f32[64,64]{1,0:T(8,128)S(1)} %reduce_sum.9), channel_id=1, source_target_pairs={{0,48},{16,64},{32,80},{48,96},{64,112},{80,128},{96,144},{112,160... | collective-permute-start | bytes 49160 | tf_op jit(solution)/shard_map/ppermute | solution.py:17
  50.8 3.3 %collective-permute-start.4 = (f32[64,64]{1,0:T(8,128)S(1)}, f32[64,64]{1,0:T(8,128)S(1)}, u32[]{:S(2)}, u32[]{:S(2)}) collective-permute-start(f32[64,64]{1,0:T(8,128)S(1)} %fusion.31), channel_id=1, source_target_pairs={{0,16},{16,0},{32,48},{48,32},{64,80},{80,64},{96,112},{112,96},{1... | collective-permute-start | bytes 49160 | tf_op jit(solution)/shard_map/ppermute | solution.py:11
  54.5 2.0 %gather_fusion = bf16[64,64,256]{2,1,0:T(8,128)(2,1)} fusion(bf16[16,64,256]{2,1,0:T(8,128)(2,1)S(1)} %copy-done.1, s32[1024]{0:T(1024)S(1)} %pad_clamp_fusion), kind=kCustom, calls=%fused_computation | custom fusion | bytes 4194560 | tf_op jit(solution)/shard_map/jit(_take)/gather | solution.py:103
  56.5 6.7 %fusion.3 = f32[16,64,256]{2,1,0:T(8,128)S(1)} fusion(bf16[16,4,256,256]{3,2,1,0:T(8,128)(2,1)} %param.13, bf16[16,4,64,256]{3,2,1,0:T(8,128)(2,1)} %bitcast.101, pred[16,4]{1,0:T(8,128)(4,1)S(1)} %copy.16), kind=kOutput, calls=%fused_computation.5 | convolution fusion | flops 537919488 | bytes 11534400 | tf_op jit(solution)/shard_map/ckrm,cknm->crn/dot_general | solution.py:107
  63.5 1.3 %collective-permute-start.8 = (f32[64,64]{1,0:T(8,128)S(1)}, f32[64,64]{1,0:T(8,128)S(1)}, u32[]{:S(2)}, u32[]{:S(2)}) collective-permute-start(f32[64,64]{1,0:T(8,128)S(1)} %add.115), channel_id=1, source_target_pairs={{96,0},{112,16},{128,32},{144,48},{160,64},{176,80},{192,96},{208,... | collective-permute-start | bytes 49160 | tf_op jit(solution)/shard_map/ppermute | solution.py:17
  65.8 1.3 %collective-permute-start.7 = (f32[64,64]{1,0:T(8,128)S(1)}, f32[64,64]{1,0:T(8,128)S(1)}, u32[]{:S(2)}, u32[]{:S(2)}) collective-permute-start(f32[64,64]{1,0:T(8,128)S(1)} %add.115), channel_id=1, source_target_pairs={{64,0},{80,16},{96,32},{112,48},{128,64},{144,80},{160,96},{176,11... | collective-permute-start | bytes 49160 | tf_op jit(solution)/shard_map/ppermute | solution.py:17
  68.0 5.5 %collective-permute-start.6 = (f32[64,64]{1,0:T(8,128)S(1)}, f32[64,64]{1,0:T(8,128)S(1)}, u32[]{:S(2)}, u32[]{:S(2)}) collective-permute-start(f32[64,64]{1,0:T(8,128)S(1)} %add.115), channel_id=1, source_target_pairs={{0,64},{16,80},{32,96},{48,112},{64,128},{80,144},{96,160},{112,17... | collective-permute-start | bytes 49160 | tf_op jit(solution)/shard_map/ppermute | solution.py:17
  76.0 2.6 %collective-permute-done.9 = f32[64,64]{1,0:T(8,128)S(1)} collective-permute-done((f32[64,64]{1,0:T(8,128)S(1)}, f32[64,64]{1,0:T(8,128)S(1)}, u32[]{:S(2)}, u32[]{:S(2)}) %collective-permute-start.9) | collective-permute-done | bytes 16416 | tf_op jit(solution)/shard_map/ppermute | solution.py:11
  78.6 7.5 %collective-permute-start.5 = (f32[64,64]{1,0:T(8,128)S(1)}, f32[64,64]{1,0:T(8,128)S(1)}, u32[]{:S(2)}, u32[]{:S(2)}) collective-permute-start(f32[64,64]{1,0:T(8,128)S(1)} %add.115), channel_id=1, source_target_pairs={{0,96},{16,112},{32,128},{48,144},{64,160},{80,176},{96,192},{112,... | collective-permute-start | bytes 49160 | tf_op jit(solution)/shard_map/ppermute | solution.py:17
  86.0 1.3 %collective-permute-start.13 = (f32[64,64]{1,0:T(8,128)S(1)}, f32[64,64]{1,0:T(8,128)S(1)}, u32[]{:S(2)}, u32[]{:S(2)}) collective-permute-start(f32[64,64]{1,0:T(8,128)S(1)} %add.123), channel_id=1, source_target_pairs={{192,0},{208,16},{224,32},{240,48},{193,1},{209,17},{225,33},{241,... | collective-permute-start | bytes 49160 | tf_op jit(solution)/shard_map/ppermute | solution.py:17
  88.3 1.3 %collective-permute-start.12 = (f32[64,64]{1,0:T(8,128)S(1)}, f32[64,64]{1,0:T(8,128)S(1)}, u32[]{:S(2)}, u32[]{:S(2)}) collective-permute-start(f32[64,64]{1,0:T(8,128)S(1)} %add.123), channel_id=1, source_target_pairs={{128,0},{144,16},{160,32},{176,48},{192,64},{208,80},{224,96},{240... | collective-permute-start | bytes 49160 | tf_op jit(solution)/shard_map/ppermute | solution.py:17
  90.6 8.5 %collective-permute-start.11 = (f32[64,64]{1,0:T(8,128)S(1)}, f32[64,64]{1,0:T(8,128)S(1)}, u32[]{:S(2)}, u32[]{:S(2)}) collective-permute-start(f32[64,64]{1,0:T(8,128)S(1)} %add.123), channel_id=1, source_target_pairs={{0,128},{16,144},{32,160},{48,176},{64,192},{80,208},{96,224},{112... | collective-permute-start | bytes 49160 | tf_op jit(solution)/shard_map/ppermute | solution.py:17
  100.0 1.3 %collective-permute-start.10 = (f32[64,64]{1,0:T(8,128)S(1)}, f32[64,64]{1,0:T(8,128)S(1)}, u32[]{:S(2)}, u32[]{:S(2)}) collective-permute-start(f32[64,64]{1,0:T(8,128)S(1)} %add.123), channel_id=1, source_target_pairs={{0,192},{16,208},{32,224},{48,240},{1,193},{17,209},{33,225},{49,2... | collective-permute-start | bytes 49160 | tf_op jit(solution)/shard_map/ppermute | solution.py:17
  109.3 3.1 %convolution_convert_fusion = bf16[128,4096]{1,0:T(8,128)(2,1)} fusion(bf16[256,4096]{1,0:T(8,128)(2,1)} %all-gather.3.cloned.1.call-done, s32[128]{0:T(128)S(1)} %eq.37, pred[128]{0:T(512)(128)(4,1)S(1)} %lt.70), kind=kOutput, calls=%fused_computation.1 | convolution fusion | flops 269025280 | bytes 3146368 | tf_op jit(solution)/shard_map/dot_general | solution.py:93
  112.3 4.3 %reshape.87 = bf16[16,8,64,64]{3,2,1,0:T(8,128)(2,1)} reshape(bf16[128,4096]{1,0:T(8,128)(2,1)} %convolution_convert_fusion) | data formatting | bytes 2097152 | tf_op jit(solution)/shard_map/reshape | solution.py:95
  116.6 2.4 %convolution_bitcast_fusion = f32[16,64,64]{2,1,0:T(8,128)S(1)} fusion(bf16[16,8,64,64]{3,2,1,0:T(8,128)(2,1)} %reshape.87, bf16[16,8,64,64]{3,2,1,0:T(8,128)(2,1)S(1)} %copy-done), kind=kOutput, calls=%fused_computation.8 | convolution fusion | flops 67108864 | bytes 2359296 | tf_op jit(solution)/shard_map/ckrb,ckab->cra/dot_general | solution.py:96
  119.0 1.6 %fusion.8 = bf16[16,64,64]{2,1,0:T(8,128)(2,1)S(1)} fusion(f32[16,64,64]{2,1,0:T(8,128)S(1)} %convolution_bitcast_fusion, f32[64,64,1]{1,0,2:T(8,128)S(1)} %convolution_bitcast_fusion.2, f32[16,64,64]{2,1,0:T(8,128)S(1)} %copy-done.2), kind=kOutput, calls=%fused_computation.11 | convolution fusion | flops 50462720 | bytes 671744 | tf_op jit(solution)/shard_map/rd,ild->irl/dot_general | solution.py:85
  (65 shorter events, 19.5 us)
Async XLA Ops:
  6.5 110.1 %copy-start = (bf16[16,8,64,64]{3,2,1,0:T(8,128)(2,1)S(1)}, bf16[16,8,64,64]{3,2,1,0:T(8,128)(2,1)}, u32[]{:S(2)}) copy-start(bf16[16,8,64,64]{3,2,1,0:T(8,128)(2,1)} %param.17) | copy-start | bytes 3145732
  6.5 47.9 %copy-start.1 = (bf16[16,64,256]{2,1,0:T(8,128)(2,1)S(1)}, bf16[16,64,256]{2,1,0:T(8,128)(2,1)}, u32[]{:S(2)}) copy-start(bf16[16,64,256]{2,1,0:T(8,128)(2,1)} %param.11) | copy-start | bytes 1572868
  6.5 47.6 %copy-start.5 = (s32[16,4]{0,1:T(4,128)S(1)}, s32[16,4]{0,1:T(4,128)}, u32[]{:S(2)}) copy-start(s32[16,4]{0,1:T(4,128)} %param.14) | copy-start | bytes 772
  6.5 102.7 %all-gather.3.cloned.1.call-start = ((), (), s32[]{:S(2)}) async-start(), calls=%async_computation | async-start | bytes 2228224 | tf_op jit(solution)/shard_map/all_gather | solution.py:90
  37.9 36.7 %collective-permute-start.3 = (f32[64,64]{1,0:T(8,128)S(1)}, f32[64,64]{1,0:T(8,128)S(1)}, u32[]{:S(2)}, u32[]{:S(2)}) collective-permute-start(f32[64,64]{1,0:T(8,128)S(1)} %reduce_sum.9), channel_id=1, source_target_pairs={{48,0},{64,16},{80,32},{96,48},{112,64},{128,80},{144,96},{160,112... | collective-permute-start | bytes 49160 | tf_op jit(solution)/shard_map/ppermute | solution.py:17
  39.2 26.6 %collective-permute-start.2 = (f32[64,64]{1,0:T(8,128)S(1)}, f32[64,64]{1,0:T(8,128)S(1)}, u32[]{:S(2)}, u32[]{:S(2)}) collective-permute-start(f32[64,64]{1,0:T(8,128)S(1)} %reduce_sum.9), channel_id=1, source_target_pairs={{32,0},{48,16},{64,32},{80,48},{96,64},{112,80},{128,96},{144,112}... | collective-permute-start | bytes 49160 | tf_op jit(solution)/shard_map/ppermute | solution.py:17
  41.2 26.8 %collective-permute-start.1 = (f32[64,64]{1,0:T(8,128)S(1)}, f32[64,64]{1,0:T(8,128)S(1)}, u32[]{:S(2)}, u32[]{:S(2)}) collective-permute-start(f32[64,64]{1,0:T(8,128)S(1)} %reduce_sum.9), channel_id=1, source_target_pairs={{0,32},{16,48},{32,64},{48,80},{64,96},{80,112},{96,128},{112,144}... | collective-permute-start | bytes 49160 | tf_op jit(solution)/shard_map/ppermute | solution.py:17
  45.6 62.5 %collective-permute-start = (f32[64,64]{1,0:T(8,128)S(1)}, f32[64,64]{1,0:T(8,128)S(1)}, u32[]{:S(2)}, u32[]{:S(2)}) collective-permute-start(f32[64,64]{1,0:T(8,128)S(1)} %reduce_sum.9), channel_id=1, source_target_pairs={{0,48},{16,64},{32,80},{48,96},{64,112},{80,128},{96,144},{112,160... | collective-permute-start | bytes 49160 | tf_op jit(solution)/shard_map/ppermute | solution.py:17
  50.8 12.7 %collective-permute-start.4 = (f32[64,64]{1,0:T(8,128)S(1)}, f32[64,64]{1,0:T(8,128)S(1)}, u32[]{:S(2)}, u32[]{:S(2)}) collective-permute-start(f32[64,64]{1,0:T(8,128)S(1)} %fusion.31), channel_id=1, source_target_pairs={{0,16},{16,0},{32,48},{48,32},{64,80},{80,64},{96,112},{112,96},{1... | collective-permute-start | bytes 49160 | tf_op jit(solution)/shard_map/ppermute | solution.py:11
  56.5 6.7 %copy-start.7 = (s32[16]{0:T(128)S(1)}, s32[16]{0:T(128)}, u32[]{:S(2)}) copy-start(s32[16]{0:T(128)} %param.16) | copy-start | bytes 196
  56.5 6.9 %copy-start.6 = (s32[16,8]{0,1:T(8,128)S(1)}, s32[16,8]{0,1:T(8,128)}, u32[]{:S(2)}) copy-start(s32[16,8]{0,1:T(8,128)} %param.15) | copy-start | bytes 1540
  56.5 52.6 %copy-start.4 = (f32[1,1,64,64]{3,2,1,0:T(8,128)S(1)}, f32[1,1,64,64]{3,2,1,0:T(8,128)}, u32[]{:S(2)}) copy-start(f32[1,1,64,64]{3,2,1,0:T(8,128)} %param.19) | copy-start | bytes 49156
  63.5 27.0 %collective-permute-start.8 = (f32[64,64]{1,0:T(8,128)S(1)}, f32[64,64]{1,0:T(8,128)S(1)}, u32[]{:S(2)}, u32[]{:S(2)}) collective-permute-start(f32[64,64]{1,0:T(8,128)S(1)} %add.115), channel_id=1, source_target_pairs={{96,0},{112,16},{128,32},{144,48},{160,64},{176,80},{192,96},{208,... | collective-permute-start | bytes 49160 | tf_op jit(solution)/shard_map/ppermute | solution.py:17
  65.8 20.3 %collective-permute-start.7 = (f32[64,64]{1,0:T(8,128)S(1)}, f32[64,64]{1,0:T(8,128)S(1)}, u32[]{:S(2)}, u32[]{:S(2)}) collective-permute-start(f32[64,64]{1,0:T(8,128)S(1)} %add.115), channel_id=1, source_target_pairs={{64,0},{80,16},{96,32},{112,48},{128,64},{144,80},{160,96},{176,11... | collective-permute-start | bytes 49160 | tf_op jit(solution)/shard_map/ppermute | solution.py:17
  68.0 20.3 %collective-permute-start.6 = (f32[64,64]{1,0:T(8,128)S(1)}, f32[64,64]{1,0:T(8,128)S(1)}, u32[]{:S(2)}, u32[]{:S(2)}) collective-permute-start(f32[64,64]{1,0:T(8,128)S(1)} %add.115), channel_id=1, source_target_pairs={{0,64},{16,80},{32,96},{48,112},{64,128},{80,144},{96,160},{112,17... | collective-permute-start | bytes 49160 | tf_op jit(solution)/shard_map/ppermute | solution.py:17
  74.6 4.0 %collective-permute-start.9 = (f32[64,64]{1,0:T(8,128)S(1)}, f32[64,64]{1,0:T(8,128)S(1)}, u32[]{:S(2)}, u32[]{:S(2)}) collective-permute-start(f32[64,64]{1,0:T(8,128)S(1)} %fusion.27), channel_id=1, source_target_pairs={{0,32},{16,48},{32,0},{48,16},{64,96},{80,112},{96,64},{112,80},{1... | collective-permute-start | bytes 49160 | tf_op jit(solution)/shard_map/ppermute | solution.py:11
  78.6 27.6 %collective-permute-start.5 = (f32[64,64]{1,0:T(8,128)S(1)}, f32[64,64]{1,0:T(8,128)S(1)}, u32[]{:S(2)}, u32[]{:S(2)}) collective-permute-start(f32[64,64]{1,0:T(8,128)S(1)} %add.115), channel_id=1, source_target_pairs={{0,96},{16,112},{32,128},{48,144},{64,160},{80,176},{96,192},{112,... | collective-permute-start | bytes 49160 | tf_op jit(solution)/shard_map/ppermute | solution.py:17
  86.0 17.2 %collective-permute-start.13 = (f32[64,64]{1,0:T(8,128)S(1)}, f32[64,64]{1,0:T(8,128)S(1)}, u32[]{:S(2)}, u32[]{:S(2)}) collective-permute-start(f32[64,64]{1,0:T(8,128)S(1)} %add.123), channel_id=1, source_target_pairs={{192,0},{208,16},{224,32},{240,48},{193,1},{209,17},{225,33},{241,... | collective-permute-start | bytes 49160 | tf_op jit(solution)/shard_map/ppermute | solution.py:17
  88.3 11.7 %collective-permute-start.12 = (f32[64,64]{1,0:T(8,128)S(1)}, f32[64,64]{1,0:T(8,128)S(1)}, u32[]{:S(2)}, u32[]{:S(2)}) collective-permute-start(f32[64,64]{1,0:T(8,128)S(1)} %add.123), channel_id=1, source_target_pairs={{128,0},{144,16},{160,32},{176,48},{192,64},{208,80},{224,96},{240... | collective-permute-start | bytes 49160 | tf_op jit(solution)/shard_map/ppermute | solution.py:17
  90.6 11.7 %collective-permute-start.11 = (f32[64,64]{1,0:T(8,128)S(1)}, f32[64,64]{1,0:T(8,128)S(1)}, u32[]{:S(2)}, u32[]{:S(2)}) collective-permute-start(f32[64,64]{1,0:T(8,128)S(1)} %add.123), channel_id=1, source_target_pairs={{0,128},{16,144},{32,160},{48,176},{64,192},{80,208},{96,224},{112... | collective-permute-start | bytes 49160 | tf_op jit(solution)/shard_map/ppermute | solution.py:17
  100.0 4.2 %collective-permute-start.10 = (f32[64,64]{1,0:T(8,128)S(1)}, f32[64,64]{1,0:T(8,128)S(1)}, u32[]{:S(2)}, u32[]{:S(2)}) collective-permute-start(f32[64,64]{1,0:T(8,128)S(1)} %add.123), channel_id=1, source_target_pairs={{0,192},{16,208},{32,224},{48,240},{1,193},{17,209},{33,225},{49,2... | collective-permute-start | bytes 49160 | tf_op jit(solution)/shard_map/ppermute | solution.py:17
  116.6 2.4 %copy-start.2 = (f32[16,64,64]{2,1,0:T(8,128)S(1)}, f32[16,64,64]{2,1,0:T(8,128)}, u32[]{:S(2)}) copy-start(f32[16,64,64]{2,1,0:T(8,128)} %param.18) | copy-start | bytes 786436
  116.6 4.0 %copy-start.3 = (bf16[16,64,256]{2,1,0:T(8,128)(2,1)S(1)}, bf16[16,64,256]{2,1,0:T(8,128)(2,1)}, u32[]{:S(2)}) copy-start(bf16[16,64,256]{2,1,0:T(8,128)(2,1)} %param.12) | copy-start | bytes 1572868
Sparse Core Ops, SparseCore 0:
  50.0 50.2 all-gather.2
